TPU v7x, 512 devices: a whole 4x4x16 slice. The times are simulated.
512 devices in a mesh: branch: 4 (over y_hi, core), segment: 8 (over y_lo, x), tp: 16 (over z).
Axes of the slice: x: 4, y: 4 (y_hi: 2, y_lo: 2; y = y_hi * 2 + y_lo), z: 16, core: 2. Of those that a mesh axis runs over, the one named last changes fastest.
Arguments:
- rollout: bfloat16 [2304, 8192], P(('branch', 'segment')), may hold values from -6 to 6
- send_rows: int32 [2304], P(('branch', 'segment')), may hold values from 0 to 71, as said below
- seq_lengths: int32 [8, 6], P('segment'), may hold values from 1 to 144, 288 in all within a row
- attn_gain: bfloat16 [4, 8192], P('branch'), may hold values from 0.099609375 to 1.8984375
- w_query: bfloat16 [4, 8192, 8192], P('branch', 'segment', 'tp'), may hold values from -1 to 1
- w_keyval: bfloat16 [4, 8192, 2048], P('branch', 'segment', 'tp'), may hold values from -1 to 1
- head_weight: bfloat16 [4, 8192], P('branch', 'tp'), may hold values from -0.0625 to 0.0625
- head_attn: bfloat16 [4, 8192], P('branch', 'tp'), may hold values from -0.25 to 0.25
Outputs:
- scores: float32 [4, 2304], P(None, ('branch', 'segment'))
Inputs may be any that keep to these rules, and one draw needn't show every extreme that they name: `send_rows`: each aligned block of 72 entries holds every number of 0 to 71 once.
All inputs are finite; a program needn't handle non-finite values.
Results may differ from a plain program's by a relative error of at most 0.006.
Values may be sent and summed in bfloat16 or wider, within the bound.
A program may use at most 128 MiB of HBM per device.

v0:
```python
import math
import jax
import jax.numpy as jnp
from jax import lax
from jax.sharding import PartitionSpec as P

HEAD = 128
HEADS = 64
KV_HEADS = 8
epsilon = 1e-05


def local(rollout, send_rows, seq_lengths, attn_gain, w_query, w_keyval, head_weight, head_attn):
    n_branch = lax.axis_size("branch")
    n_segment = lax.axis_size("segment")
    gen_rows = rollout.shape[0]
    piece_rows = gen_rows // n_segment
    row_width = rollout.shape[1]
    ordered = jnp.take(rollout, send_rows, axis=0).reshape(n_segment, piece_rows, row_width)
    copies = jnp.broadcast_to(ordered[None], (n_branch, n_segment, piece_rows, row_width))
    copies = copies.reshape(n_branch * n_segment, piece_rows, row_width)
    arrived = lax.all_to_all(copies, ("branch", "segment"), split_axis=0, concat_axis=0, tiled=True)
    packed = arrived.reshape(-1, row_width)
    pack_rows = packed.shape[0]
    rows_float = packed.astype(jnp.float32)
    mean_square = jnp.mean(rows_float * rows_float, axis=-1, keepdims=True)
    normed = (
        rows_float * lax.rsqrt(mean_square + epsilon) * attn_gain[0].astype(jnp.float32)
    ).astype(jnp.bfloat16)
    query_acc = jnp.dot(
        normed,
        lax.all_gather(w_query, "segment", axis=1, tiled=True)[0],
        preferred_element_type=jnp.float32,
    )
    keyval_acc = jnp.dot(
        normed,
        lax.all_gather(w_keyval, "segment", axis=1, tiled=True)[0],
        preferred_element_type=jnp.float32,
    )
    queries = query_acc.astype(jnp.bfloat16)
    keyval_part = keyval_acc.astype(jnp.bfloat16)
    keyval = lax.all_gather(keyval_part, "tp", axis=1, tiled=True)
    tp_index = lax.axis_index("tp")
    heads_here = queries.shape[1] // HEAD
    group_size = HEADS // KV_HEADS
    per_group = min(heads_here, group_size)
    group_span = heads_here // per_group
    kv_first = tp_index * heads_here // group_size
    key_rows = lax.dynamic_slice_in_dim(keyval, kv_first * HEAD, group_span * HEAD, 1)
    value_rows = lax.dynamic_slice_in_dim(
        keyval, KV_HEADS * HEAD + kv_first * HEAD, group_span * HEAD, 1
    )
    key_rows = key_rows.reshape(pack_rows, group_span, HEAD)
    value_rows = value_rows.reshape(pack_rows, group_span, HEAD)
    queries = queries.reshape(pack_rows, group_span, per_group, HEAD)
    positions = jnp.arange(pack_rows, dtype=jnp.int32)
    doc_ends = jnp.cumsum(seq_lengths[0])
    doc_ids = jnp.sum((positions[:, None] >= doc_ends[None, :]).astype(jnp.int32), axis=-1)
    visible = (doc_ids[:, None] == doc_ids[None, :]) & (positions[None, :] <= positions[:, None])
    logits = jnp.einsum(
        "qgpc,kgc->gpqk", queries, key_rows, preferred_element_type=jnp.float32
    ) / math.sqrt(HEAD)
    logits = jnp.where(visible[None, None], logits, -1e30)
    row_max = jnp.max(logits, axis=-1, keepdims=True)
    expo = jnp.exp(logits - row_max)
    probabilities = (expo / jnp.sum(expo, axis=-1, keepdims=True)).astype(jnp.bfloat16)
    attended = jnp.einsum(
        "gpqk,kgc->qgpc", probabilities, value_rows, preferred_element_type=jnp.float32
    )
    attended = attended.reshape(pack_rows, heads_here * HEAD)
    slice_width = head_weight.shape[1]
    own_columns = lax.dynamic_slice_in_dim(packed, tp_index * slice_width, slice_width, 1)
    direct = jnp.dot(own_columns, head_weight[0], preferred_element_type=jnp.float32)
    through = jnp.dot(attended, head_attn[0].astype(jnp.float32), precision=lax.Precision.HIGHEST)
    totals = lax.psum(direct + through, "tp")
    outgoing = totals.reshape(n_branch * n_segment, piece_rows)
    incoming = lax.all_to_all(
        outgoing, ("branch", "segment"), split_axis=0, concat_axis=0, tiled=True
    )
    incoming = incoming.reshape(n_branch, n_segment * piece_rows)
    scores = jnp.zeros((n_branch, gen_rows), jnp.float32).at[:, send_rows].set(incoming)
    return scores


def solution(mesh):
    return jax.shard_map(
        local,
        mesh=mesh,
        in_specs=(
            P(("branch", "segment"), None),
            P(("branch", "segment")),
            P("segment", None),
            P("branch", None),
            P("branch", "segment", "tp"),
            P("branch", "segment", "tp"),
            P("branch", "tp"),
            P("branch", "tp"),
        ),
        out_specs=P(None, ("branch", "segment")),
        check_vma=False,
    )
```

profile of v0, /device:TPU:1, one launch (start us, length us, event | category | flops | bytes accessed | tf_op | source)
XLA Modules:
  0.0 387.5 jit_solution(12303742169167186144)
XLA Ops:
  6.5 0.0 copy-start
  6.5 0.0 all-gather.4.cloned.1.call-start
  6.5 0.7 all-gather.4.cloned.1.call-update
  7.3 0.0 all-gather.8.cloned.1.call-start
  7.3 0.7 all-gather.8.cloned.1.call-update
  8.0 0.7 compare_select_fusion
  8.7 0.0 copy-done
  8.7 2.4 gather_fusion
  11.1 1.8 gather.7
  12.9 0.0 copy-done.4
  12.9 0.1 broadcast_in_dim.48
  13.0 0.3 broadcast_select_fusion
  13.3 4.4 %broadcast_in_dim.51 = bf16[4,8,9,8192]{3,2,1,0:T(8,128)(2,1)} broadcast(bf16[8,9,8192]{2,1,0:T(8,128)(2,1)S(1)} %broadcast_select_fusion), dimensions={1,2,3} | broadcast | bytes 5898240 | tf_op jit(solution)/shard_map/broadcast_in_dim | solution.py:20
  17.7 11.6 %all-to-all-start = ((bf16[32,9,8192]{2,1,0:T(8,128)(2,1)}), bf16[32,9,8192]{2,1,0:T(8,128)(2,1)}, u32[]{:S(2)}, u32[]{:S(2)}) async-start(bf16[32,9,8192]{2,1,0:T(8,128)(2,1)} %bitcast.58), calls=%async_computation | async-start | bytes 16777216 | tf_op jit(solution)/shard_map/all_to_all | solution.py:22
  29.4 0.2 all-gather.6.cloned.1.call-start
  29.6 0.0 copy-done.1
  29.6 144.8 %all-to-all-done = bf16[32,9,8192]{2,1,0:T(8,128)(2,1)} async-done(((bf16[32,9,8192]{2,1,0:T(8,128)(2,1)}), bf16[32,9,8192]{2,1,0:T(8,128)(2,1)}, u32[]{:S(2)}, u32[]{:S(2)}) %all-to-all-start) | async-done | bytes 4718624 | tf_op jit(solution)/shard_map/all_to_all | solution.py:22
  174.5 5.4 %fusion = f32[32,9]{1,0:T(8,128)S(1)} fusion(bf16[32,9,8192]{2,1,0:T(8,128)(2,1)} %all-to-all-done), kind=kLoop, calls=%fused_computation.4 | loop fusion | flops 7077600 | bytes 4719744 | tf_op jit(solution)/shard_map/reduce_sum | solution.py:26
  179.9 9.9 %fusion.2 = bf16[32,9,8192]{2,1,0:T(8,128)(2,1)} fusion(bf16[32,9,8192]{2,1,0:T(8,128)(2,1)} %all-to-all-done, f32[8192]{0:T(1024)S(1)} %bitcast.60, f32[32,9]{1,0:T(8,128)S(1)} %add_rsqrt_fusion), kind=kLoop, calls=%fused_computation.6 | loop fusion | flops 9437184 | bytes 9471104 | tf_op jit(solution)/shard_map/convert_element_type | solution.py:29
  189.9 6.9 %convert_element_type.30 = bf16[288,8192]{1,0:T(8,128)(2,1)} reshape(bf16[32,9,8192]{2,1,0:T(8,128)(2,1)} %fusion.2) | data formatting | bytes 9437184 | tf_op jit(solution)/shard_map/convert_element_type | solution.py:29
  196.8 5.1 %fusion.14 = bf16[288,128]{1,0:T(8,128)(2,1)} fusion(bf16[288,8192]{1,0:T(8,128)(2,1)} %convert_element_type.30, bf16[1,8192,128]{2,1,0:T(8,128)(2,1)} %all-gather.4.cloned.1.call-done), kind=kOutput, calls=%fused_computation.19 | convolution fusion | flops 604016640 | bytes 6889472 | tf_op jit(solution)/shard_map/dot_general | solution.py:35
  202.0 0.0 all-gather.6.cloned.1.call-update
  202.0 0.0 copy-done.5
  202.0 0.2 reduce-window.8
  202.2 0.1 convert_reduce_fusion
  202.3 0.1 fusion.20
  202.4 0.0 copy-start.2
  202.4 6.9 %reshape.163 = bf16[288,8192]{1,0:T(8,128)(2,1)} reshape(bf16[32,9,8192]{2,1,0:T(8,128)(2,1)} %all-to-all-done) | data formatting | bytes 9437184 | tf_op jit(solution)/shard_map/reshape | solution.py:23
  209.3 0.0 copy-done.2
  209.3 1.2 convolution_reduce_fusion.1
  210.5 17.9 %all-gather.8.cloned.1.call-done = bf16[1,8192,512]{2,1,0:T(8,128)(2,1)} async-done(((bf16[1,1024,512]{2,1,0:T(8,128)(2,1)}), bf16[1,8192,512]{2,1,0:T(8,128)(2,1)}) %all-gather.8.cloned.1.call-update) | async-done | bytes 8388624 | tf_op jit(solution)/shard_map/all_gather | solution.py:32
  228.4 7.4 %fusion.11 = bf16[36,4,8,128]{3,2,1,0:T(8,128)(2,1)S(1)} fusion(bf16[288,8192]{1,0:T(8,128)(2,1)} %convert_element_type.30, bf16[1,8192,512]{2,1,0:T(8,128)(2,1)} %all-gather.8.cloned.1.call-done), kind=kOutput, calls=%fused_computation.18 | convolution fusion | flops 2416066560 | bytes 13402112 | tf_op jit(solution)/shard_map/dot_general | solution.py:30
  235.8 58.6 %all-gather.6.cloned.1.call-done = bf16[288,2048]{1,0:T(8,128)(2,1)} async-done(((bf16[288,128]{1,0:T(8,128)(2,1)}), bf16[288,2048]{1,0:T(8,128)(2,1)}) %all-gather.6.cloned.1.call-update) | async-done | bytes 1179664 | tf_op jit(solution)/shard_map/all_gather | solution.py:42
  294.4 1.4 fusion.35
  295.8 0.3 fusion.7
  296.1 0.0 copy-start.3
  296.1 1.5 convolution_bitcast_fusion
  297.5 0.4 copy.25
  297.9 0.4 convolution_reduce_fusion
  298.4 0.1 all_to_all.10
  298.5 40.6 %psum.7 = f32[32,1,9]{2,0,1:T(8,128)S(1)} all-reduce(f32[32,1,9]{2,0,1:T(8,128)S(1)} %all_to_all.10), channel_id=1, replica_groups=mesh['branch'=4,'segment'=8,'tp'=16] {'tp'}, use_global_device_ids=true, to_apply=%region_5.6 | all-reduce | flops 288 | bytes 2304 | tf_op jit(solution)/shard_map/psum | solution.py:75
  339.0 39.1 %all_to_all.14 = f32[32,1,9]{2,1,0:T(1,128)S(1)} all-to-all(f32[32,1,9]{2,1,0:T(1,128)S(1)} %bitcast.61), channel_id=1, replica_groups=mesh['branch'=4,'segment'=8,'tp'=16] {'branch','segment'}, dimensions={0} | all-to-all | bytes 2304 | tf_op jit(solution)/shard_map/all_to_all | solution.py:77
  378.2 0.5 broadcast.79
  378.7 0.7 reduce.10
  379.4 0.1 reshape.180
  379.4 0.1 copy.27
  379.6 0.7 scatter_custom_fusion
  380.3 0.7 copy.28
  (10 shorter events, 0.1 us)
Async XLA Ops:
  6.5 2.1 copy-start
  6.5 190.3 %all-gather.4.cloned.1.call-start = ((), (), s32[]{:S(2)}) async-start(), calls=%async_computation.2 | async-start | bytes 2359296 | tf_op jit(solution)/shard_map/all_gather | solution.py:37
  7.3 221.2 %all-gather.8.cloned.1.call-start = ((), (), s32[]{:S(2)}) async-start(), calls=%async_computation.4 | async-start | bytes 9437184 | tf_op jit(solution)/shard_map/all_gather | solution.py:32
  11.1 1.8 copy-start.4
  17.7 11.9 %copy-start.1 = (bf16[1,8192]{1,0:T(2,128)(2,1)S(1)}, bf16[1,8192]{1,0:T(2,128)(2,1)}, u32[]{:S(2)}) copy-start(bf16[1,8192]{1,0:T(2,128)(2,1)} %param.11) | copy-start | bytes 49156
  17.7 156.7 %all-to-all-start = ((bf16[32,9,8192]{2,1,0:T(8,128)(2,1)}), bf16[32,9,8192]{2,1,0:T(8,128)(2,1)}, u32[]{:S(2)}, u32[]{:S(2)}) async-start(bf16[32,9,8192]{2,1,0:T(8,128)(2,1)} %bitcast.58), calls=%async_computation | async-start | bytes 16777216 | tf_op jit(solution)/shard_map/all_to_all | solution.py:22
  29.4 265.0 %all-gather.6.cloned.1.call-start = ((), (), s32[]{:S(2)}) async-start(), calls=%async_computation.3 | async-start | bytes 1253376 | tf_op jit(solution)/shard_map/all_gather | solution.py:42
  196.8 5.2 %copy-start.5 = (s32[1,6]{1,0:T(1,128)S(1)}, s32[1,6]{1,0:T(1,128)}, u32[]{:S(2)}) copy-start(s32[1,6]{1,0:T(1,128)} %param.10) | copy-start | bytes 76
  202.4 6.9 %copy-start.2 = (bf16[1,512]{1,0:T(2,128)(2,1)S(1)}, bf16[1,512]{1,0:T(2,128)(2,1)}, u32[]{:S(2)}) copy-start(bf16[1,512]{1,0:T(2,128)(2,1)} %param.14) | copy-start | bytes 3076
  296.1 1.9 copy-start.3
Sparse Core Ops, SparseCore 0:
  9.4 92.1 all-gather.3
  103.7 124.6 all-gather.7
  230.4 63.9 all-gather.5
where the time goes:
time: 388 us; the launch traced here: 387 us
  waiting for transfers between devices  223 us (57%)
  blocking collectives  79.7 us (21%)
  local copies, waits for them, and re-layouts  25.2 us (6%)
  other arithmetic  17.7 us (5%)
  matrix products  17 us (4%)
  between operations  13.3 us (3%)
  starting transfers between devices  11.9 us (3%)
    all_to_all x1, waiting for transfers between devices, local(): lax.all_to_all(copies, ('branch', 'segment'), split_axis=0, concat_axis=0...  145 us
    all_gather x1, waiting for transfers between devices, local(): keyval = lax.all_gather(keyval_part, 'tp', axis=1, tiled=True)  58.6 us
    psum x1, blocking collectives, local(): totals = lax.psum(direct + through, 'tp')  40.6 us
    all_to_all x1, blocking collectives, local(): lax.all_to_all(outgoing, ('branch', 'segment'), split_axis=0, concat_axis...  39.1 us
    all_gather x1, waiting for transfers between devices, local(): lax.all_gather(w_query, 'segment', axis=1, tiled=True)[0]  17.9 us
    all_to_all x1, starting transfers between devices, local(): lax.all_to_all(copies, ('branch', 'segment'), split_axis=0, concat_axis=0...  11.6 us
    convert_element_type x1, other arithmetic, local(): normed = (rows_float * lax.rsqrt(mean_square + epsilon) * attn_gain[0].as...  9.94 us
  transfers between devices with their start and end apart: 4, of which 3 were waited for; matrix products, arithmetic and copies ran while one was open for 14% of the time, Pallas kernels for 0%

commit v1 on v0

--- a/solution.py
+++ b/solution.py
@@ -39,7 +39,11 @@
     )
     queries = query_acc.astype(jnp.bfloat16)
     keyval_part = keyval_acc.astype(jnp.bfloat16)
-    keyval = lax.all_gather(keyval_part, "tp", axis=1, tiled=True)
+    size = lax.axis_size("tp")
+    repeats = [size if d == 1 else 1 for d in range(keyval_part.ndim)]
+    keyval = lax.all_to_all(
+        jnp.tile(keyval_part, repeats), "tp", split_axis=1, concat_axis=1, tiled=True
+    )
     tp_index = lax.axis_index("tp")
     heads_here = queries.shape[1] // HEAD
     group_size = HEADS // KV_HEADS

time: 388 us -> 364 us (0.938)
  waiting for transfers between devices: 223 us -> 190 us
  starting transfers between devices: 11.9 us -> 26.4 us
  blocking collectives: 79.7 us -> 73.8 us
    all_gather x1 -> x0, waiting for transfers between devices: 58.6 us -> none  [local(): keyval = lax.all_gather(keyval_part, 'tp', axis=1, tiled=True)]
    all_to_all x0 -> x1, waiting for transfers between devices: none -> 41.7 us  [local(): lax.all_to_all(jnp.tile(keyval_part, repeats), 'tp', split_axis=1, concat...]
    all_gather x1, waiting for transfers between devices: 17.9 us -> 0.02 us  [local(): lax.all_gather(w_query, 'segment', axis=1, tiled=True)[0]]
    all_to_all x0 -> x1, starting transfers between devices: none -> 14.8 us  [local(): lax.all_to_all(jnp.tile(keyval_part, repeats), 'tp', split_axis=1, concat...]
    all_to_all x1, blocking collectives: 39.1 us -> 29.5 us  [local(): lax.all_to_all(outgoing, ('branch', 'segment'), split_axis=0, concat_axis...]
  transfers between devices with their start and end apart: 4 -> 4, of which waited for: 3 -> 2; matrix products, arithmetic and copies ran while one was open for 14% -> 13% of each run, Pallas kernels for 0% -> 0%
where the time goes in v1:
time: 364 us
  waiting for transfers between devices  190 us (52%)
  blocking collectives  73.8 us (20%)
  local copies, waits for them, and re-layouts  26.5 us (7%)
  starting transfers between devices  26.4 us (7%)
  other arithmetic  19 us (5%)
  matrix products  14.5 us (4%)
  between operations  13.6 us (4%)
    all_to_all x1, waiting for transfers between devices, local(): lax.all_to_all(copies, ('branch', 'segment'), split_axis=0, concat_axis=0...  147 us
    psum x1, blocking collectives, local(): totals = lax.psum(direct + through, 'tp')  44.3 us
    all_to_all x1, waiting for transfers between devices, local(): lax.all_to_all(jnp.tile(keyval_part, repeats), 'tp', split_axis=1, concat...  41.7 us
    all_to_all x1, blocking collectives, local(): lax.all_to_all(outgoing, ('branch', 'segment'), split_axis=0, concat_axis...  29.5 us
    all_to_all x1, starting transfers between devices, local(): lax.all_to_all(jnp.tile(keyval_part, repeats), 'tp', split_axis=1, concat...  14.8 us
    all_to_all x1, starting transfers between devices, local(): lax.all_to_all(copies, ('branch', 'segment'), split_axis=0, concat_axis=0...  11.6 us
    convert_element_type x1, other arithmetic, local(): normed = (rows_float * lax.rsqrt(mean_square + epsilon) * attn_gain[0].as...  9.93 us
    dot_general x1, matrix products, local(): jnp.dot(normed, lax.all_gather(w_query, 'segment', axis=1, tiled=True)[0]...  7.43 us
  transfers between devices with their start and end apart: 4, of which 2 were waited for; matrix products, arithmetic and copies ran while one was open for 13% of the time, Pallas kernels for 0%

profile of v1, /device:TPU:1, one launch (start us, length us, event | category | flops | bytes accessed | tf_op | source)
XLA Modules:
  0.0 363.8 jit_solution(10233151507386744609)
XLA Ops:
  6.5 0.0 copy-start
  6.5 0.7 all-gather.3.cloned.1.call-update
  7.3 0.0 all-gather.5.cloned.1.call-start
  7.3 0.7 all-gather.5.cloned.1.call-update
  8.0 0.7 compare_select_fusion
  8.7 0.7 compare_and_fusion
  9.3 0.0 copy-done
  9.3 2.4 gather_fusion
  11.7 1.8 gather.7
  13.6 0.1 broadcast_in_dim.48
  13.7 0.3 broadcast_select_fusion
  13.9 4.4 %broadcast_in_dim.51 = bf16[4,8,9,8192]{3,2,1,0:T(8,128)(2,1)} broadcast(bf16[8,9,8192]{2,1,0:T(8,128)(2,1)S(1)} %broadcast_select_fusion), dimensions={1,2,3} | broadcast | bytes 5898240 | tf_op jit(solution)/shard_map/broadcast_in_dim | solution.py:20
  18.4 11.6 %all-to-all-start = ((bf16[32,9,8192]{2,1,0:T(8,128)(2,1)}), bf16[32,9,8192]{2,1,0:T(8,128)(2,1)}, u32[]{:S(2)}, u32[]{:S(2)}) async-start(bf16[32,9,8192]{2,1,0:T(8,128)(2,1)} %bitcast.63), calls=%async_computation | async-start | bytes 16777216 | tf_op jit(solution)/shard_map/all_to_all | solution.py:22
  30.0 0.0 copy-done.2
  30.0 146.7 %all-to-all-done = bf16[32,9,8192]{2,1,0:T(8,128)(2,1)} async-done(((bf16[32,9,8192]{2,1,0:T(8,128)(2,1)}), bf16[32,9,8192]{2,1,0:T(8,128)(2,1)}, u32[]{:S(2)}, u32[]{:S(2)}) %all-to-all-start) | async-done | bytes 4718624 | tf_op jit(solution)/shard_map/all_to_all | solution.py:22
  176.7 5.4 %fusion = f32[32,9]{1,0:T(8,128)S(1)} fusion(bf16[32,9,8192]{2,1,0:T(8,128)(2,1)} %all-to-all-done), kind=kLoop, calls=%fused_computation.4 | loop fusion | flops 7077600 | bytes 4719744 | tf_op jit(solution)/shard_map/reduce_sum | solution.py:26
  182.2 9.9 %fusion.2 = bf16[32,9,8192]{2,1,0:T(8,128)(2,1)} fusion(bf16[32,9,8192]{2,1,0:T(8,128)(2,1)} %all-to-all-done, f32[8192]{0:T(1024)S(1)} %bitcast.65, f32[32,9]{1,0:T(8,128)S(1)} %add_rsqrt_fusion), kind=kLoop, calls=%fused_computation.6 | loop fusion | flops 9437184 | bytes 9471104 | tf_op jit(solution)/shard_map/convert_element_type | solution.py:29
  192.1 7.0 %convert_element_type.30 = bf16[288,8192]{1,0:T(8,128)(2,1)} reshape(bf16[32,9,8192]{2,1,0:T(8,128)(2,1)} %fusion.2) | data formatting | bytes 9437184 | tf_op jit(solution)/shard_map/convert_element_type | solution.py:29
  199.1 4.5 %fusion.14 = bf16[288,128]{1,0:T(8,128)(2,1)S(1)} fusion(bf16[288,8192]{1,0:T(8,128)(2,1)} %convert_element_type.30, bf16[1,8192,128]{2,1,0:T(8,128)(2,1)} %all-gather.3.cloned.1.call-done), kind=kOutput, calls=%fused_computation.20 | convolution fusion | flops 604016640 | bytes 6889472 | tf_op jit(solution)/shard_map/dot_general | solution.py:35
  203.6 0.0 copy-start.5
  203.6 1.2 tile.2
  204.8 14.8 %all-to-all-start.1 = ((bf16[288,16,128]{2,0,1:T(8,128)(2,1)}), bf16[288,16,128]{2,0,1:T(8,128)(2,1)S(1)}, u32[]{:S(2)}, u32[]{:S(2)}) async-start(bf16[288,16,128]{2,0,1:T(8,128)(2,1)} %tile.2), calls=%async_computation.1 | async-start | bytes 2359296 | tf_op jit(solution)/shard_map/all_to_all | solution.py:44
  219.6 0.2 reduce-window.8
  219.8 0.1 convert_reduce_fusion
  219.9 0.8 fusion.20
  220.7 6.8 %reshape.170 = bf16[288,8192]{1,0:T(8,128)(2,1)} reshape(bf16[32,9,8192]{2,1,0:T(8,128)(2,1)} %all-to-all-done) | data formatting | bytes 9437184 | tf_op jit(solution)/shard_map/reshape | solution.py:23
  227.5 0.0 copy-done.3
  227.5 1.2 convolution_reduce_fusion.1
  228.7 41.7 %all-to-all-done.1 = bf16[288,16,128]{2,0,1:T(8,128)(2,1)S(1)} async-done(((bf16[288,16,128]{2,0,1:T(8,128)(2,1)}), bf16[288,16,128]{2,0,1:T(8,128)(2,1)S(1)}, u32[]{:S(2)}, u32[]{:S(2)}) %all-to-all-start.1) | async-done | bytes 1179680 | tf_op jit(solution)/shard_map/all_to_all | solution.py:44
  270.4 0.1 copy_bitcast_fusion
  270.6 0.0 copy-start.1
  270.6 0.0 all-gather.5.cloned.1.call-done
  270.6 7.4 %fusion.11 = bf16[36,4,8,128]{3,2,1,0:T(8,128)(2,1)S(1)} fusion(bf16[288,8192]{1,0:T(8,128)(2,1)} %convert_element_type.30, bf16[1,8192,512]{2,1,0:T(8,128)(2,1)} %all-gather.5.cloned.1.call-done), kind=kOutput, calls=%fused_computation.19 | convolution fusion | flops 2416066560 | bytes 13402112 | tf_op jit(solution)/shard_map/dot_general | solution.py:30
  278.1 0.5 fusion.35
  278.5 0.3 fusion.7
  278.8 0.0 copy-start.4
  278.8 0.6 convolution_bitcast_fusion
  279.4 0.4 copy.27
  279.8 0.4 convolution_reduce_fusion
  280.2 0.1 all_to_all.18
  280.4 44.3 %psum.7 = f32[32,1,9]{2,0,1:T(8,128)S(1)} all-reduce(f32[32,1,9]{2,0,1:T(8,128)S(1)} %all_to_all.18), channel_id=1, replica_groups=mesh['branch'=4,'segment'=8,'tp'=16] {'tp'}, use_global_device_ids=true, to_apply=%region_5.6 | all-reduce | flops 288 | bytes 2304 | tf_op jit(solution)/shard_map/psum | solution.py:79
  324.7 29.5 %all_to_all.23 = f32[32,1,9]{2,1,0:T(1,128)S(1)} all-to-all(f32[32,1,9]{2,1,0:T(1,128)S(1)} %bitcast.66), channel_id=1, replica_groups=mesh['branch'=4,'segment'=8,'tp'=16] {'branch','segment'}, dimensions={0} | all-to-all | bytes 2304 | tf_op jit(solution)/shard_map/all_to_all | solution.py:81
  354.2 0.5 broadcast.82
  354.7 0.7 reduce.10
  355.4 0.1 reshape.187
  355.5 0.1 copy.29
  355.6 0.7 scatter_custom_fusion
  356.3 0.7 copy.30
  (11 shorter events, 0.1 us)
Async XLA Ops:
  6.5 2.8 copy-start
  6.5 192.6 %all-gather.3.cloned.1.call-start = ((), (), s32[]{:S(2)}) async-start(), calls=%async_computation.3 | async-start | bytes 2359296 | tf_op jit(solution)/shard_map/all_gather | solution.py:37
  7.3 263.3 %all-gather.5.cloned.1.call-start = ((), (), s32[]{:S(2)}) async-start(), calls=%async_computation.4 | async-start | bytes 9437184 | tf_op jit(solution)/shard_map/all_gather | solution.py:32
  18.4 11.6 %copy-start.2 = (bf16[1,8192]{1,0:T(2,128)(2,1)S(1)}, bf16[1,8192]{1,0:T(2,128)(2,1)}, u32[]{:S(2)}) copy-start(bf16[1,8192]{1,0:T(2,128)(2,1)} %param.11) | copy-start | bytes 49156
  18.4 158.4 %all-to-all-start = ((bf16[32,9,8192]{2,1,0:T(8,128)(2,1)}), bf16[32,9,8192]{2,1,0:T(8,128)(2,1)}, u32[]{:S(2)}, u32[]{:S(2)}) async-start(bf16[32,9,8192]{2,1,0:T(8,128)(2,1)} %bitcast.63), calls=%async_computation | async-start | bytes 16777216 | tf_op jit(solution)/shard_map/all_to_all | solution.py:22
  203.6 16.0 %copy-start.5 = (s32[1,6]{1,0:T(1,128)S(1)}, s32[1,6]{1,0:T(1,128)}, u32[]{:S(2)}) copy-start(s32[1,6]{1,0:T(1,128)} %param.10) | copy-start | bytes 76
  204.8 65.6 %all-to-all-start.1 = ((bf16[288,16,128]{2,0,1:T(8,128)(2,1)}), bf16[288,16,128]{2,0,1:T(8,128)(2,1)S(1)}, u32[]{:S(2)}, u32[]{:S(2)}) async-start(bf16[288,16,128]{2,0,1:T(8,128)(2,1)} %tile.2), calls=%async_computation.1 | async-start | bytes 2359296 | tf_op jit(solution)/shard_map/all_to_all | solution.py:44
  220.7 6.8 %copy-start.3 = (bf16[1,512]{1,0:T(2,128)(2,1)S(1)}, bf16[1,512]{1,0:T(2,128)(2,1)}, u32[]{:S(2)}) copy-start(bf16[1,512]{1,0:T(2,128)(2,1)} %param.14) | copy-start | bytes 3076
  270.6 7.5 %copy-start.1 = (pred[288,288]{0,1:T(8,128)(4,1)S(1)}, pred[288,288]{0,1:T(8,128)(4,1)}, u32[]{:S(2)}) copy-start(pred[288,288]{0,1:T(8,128)(4,1)} %fusion.20) | copy-start | bytes 248836
  278.8 1.0 copy-start.4
Sparse Core Ops, SparseCore 0:
  9.4 86.7 all-gather.2
  98.3 130.1 all-gather.4
